TPU v7x, 1024 devices: a whole 8x8x8 slice. The times are simulated.
1024 devices in a mesh: rows: 64 (over y, z_hi, core), vecs: 16 (over x, z_lo).
Axes of the slice: x: 8, y: 8, z: 8 (z_hi: 4, z_lo: 2; z = z_hi * 2 + z_lo), core: 2. Of those that a mesh axis runs over, the one named last changes fastest.
Arguments:
- eigvecs: bfloat16 [65536, 4096], P('rows', 'vecs'), may hold values from -6 to 6
- reflectors: bfloat16 [2, 65536, 1024], P(None, 'rows', 'vecs'), may hold values from -0.125 to 0.125
- factors: bfloat16 [2, 1024, 1024], replicated, as said below
Outputs:
- back_vecs: bfloat16 [65536, 4096], P('rows', 'vecs')
Inputs may be any that keep to these rules, and one draw needn't show every extreme that they name: `factors`: each factor is upper triangular, its diagonal between 0.15 and 0.35.
All inputs are finite; a program needn't handle non-finite values.
Results may differ from a plain program's by a relative error of at most 0.01.
Values may be sent and summed in bfloat16 or wider, within the bound.
A program may use at most 32 MiB of HBM per device.

v0:
```python
import jax
import jax.numpy as jnp
from jax import lax
from jax.sharding import PartitionSpec as P


def body(eigvecs, reflectors, factors):
    current = eigvecs
    for which in (1, 0):
        panel = lax.all_gather(reflectors[which], "vecs", axis=1, tiled=True)
        partial_value = lax.dot_general(
            panel, current, (((0,), (0,)), ((), ())), preferred_element_type=jnp.float32
        )
        coeff = lax.psum(partial_value, "rows").astype(jnp.bfloat16)
        scaled = jnp.dot(factors[which], coeff, preferred_element_type=jnp.float32).astype(
            jnp.bfloat16
        )
        update = jnp.dot(panel, scaled, preferred_element_type=jnp.float32)
        current = (current.astype(jnp.float32) - update).astype(jnp.bfloat16)
    return current


def solution(mesh):
    in_specs = (P("rows", "vecs"), P(None, "rows", "vecs"), P())
    out_specs = P("rows", "vecs")
    return jax.shard_map(body, mesh=mesh, in_specs=in_specs, out_specs=out_specs, check_vma=False)
```

profile of v0, /device:TPU:1, one launch (start us, length us, event | category | flops | bytes accessed | tf_op | source)
XLA Modules:
  0.0 685.9 jit_solution(429126618923675934)
XLA Ops:
  6.5 0.0 all-gather.5.cloned.1.call-start
  6.5 1.7 fusion.49
  8.2 0.0 all-gather.5.cloned.1.call-update
  8.2 0.0 all-gather.7.cloned.1.call-start
  8.3 0.7 all-gather.7.cloned.1.call-update
  9.0 1.2 copy.4
  10.2 80.0 %all-gather.5.cloned.1.call-done = bf16[1,1024,1024]{1,2,0:T(8,128)(2,1)} async-done(((bf16[1,1024,64]{1,2,0:T(8,128)(2,1)}), bf16[1,1024,1024]{1,2,0:T(8,128)(2,1)}) %all-gather.5.cloned.1.call-update) | async-done | bytes 2097168 | tf_op jit(solution)/shard_map/all_gather | solution.py:10
  90.2 2.4 fusion.10
  92.6 291.1 %all-reduce.2 = bf16[1024,256]{1,0:T(8,128)(2,1)S(1)} all-reduce(f32[1024,256]{1,0:T(8,128)S(1)} %fusion.10), channel_id=1, replica_groups=mesh['rows'=64,'vecs'=16] {'rows'}, use_global_device_ids=true, to_apply=%region_0.0 | all-reduce | flops 262144 | bytes 1572864 | tf_op jit(solution)/shard_map/psum | solution.py:14
  383.7 4.3 fusion.35
  388.0 0.0 all-gather.7.cloned.1.call-done
  388.0 0.0 copy-start
  388.0 2.6 fusion.17
  390.7 284.2 %all-reduce.3 = bf16[1024,256]{0,1:T(8,128)(2,1)} all-reduce(f32[1024,256]{0,1:T(8,128)S(1)} %fusion.17), channel_id=1, replica_groups=mesh['rows'=64,'vecs'=16] {'rows'}, use_global_device_ids=true, to_apply=%region_1.0 | all-reduce | flops 262144 | bytes 1572864 | tf_op jit(solution)/shard_map/psum | solution.py:14
  674.9 0.0 copy-done
  674.9 3.1 fusion.38
  678.0 1.0 copy.5
Async XLA Ops:
  6.5 83.7 %all-gather.5.cloned.1.call-start = ((), (), s32[]{:S(2)}) async-start(), calls=%async_computation | async-start | bytes 2228224 | tf_op jit(solution)/shard_map/all_gather | solution.py:10
  8.2 379.8 %all-gather.7.cloned.1.call-start = ((), (), s32[]{:S(2)}) async-start(), calls=%async_computation.1 | async-start | bytes 2228224 | tf_op jit(solution)/shard_map/all_gather | solution.py:10
  388.0 286.9 %copy-start = (bf16[1,1024,1024]{1,2,0:T(8,128)(2,1)S(1)}, bf16[1,1024,1024]{1,2,0:T(8,128)(2,1)}, u32[]{:S(2)}) copy-start(bf16[1,1024,1024]{1,2,0:T(8,128)(2,1)} %all-gather.7.cloned.1.call-done) | copy-start | bytes 6291460
Sparse Core Ops, SparseCore 0:
  10.0 80.1 all-gather.4
  92.9 78.0 all-gather.6
where the time goes:
time: 695 us; the launch traced here: 686 us
  blocking collectives  575 us (83%)
  waiting for transfers between devices  80.7 us (12%)
  between operations  13.4 us (2%)
  matrix products  12.5 us (2%)
    psum x2, blocking collectives, body(): coeff = lax.psum(partial_value, 'rows').astype(jnp.bfloat16)  575 us
    all_gather x2, waiting for transfers between devices, body(): panel = lax.all_gather(reflectors[which], 'vecs', axis=1, tiled=True)  80 us
  transfers between devices with their start and end apart: 2, of which 1 were waited for; matrix products, arithmetic and copies ran while one was open for 1% of the time, Pallas kernels for 0%

commit v1 on v0

v1 whole, which is shorter than its diff:
```python
import jax
import jax.numpy as jnp
from jax import lax
from jax.experimental import pallas as pl
from jax.experimental.pallas import tpu as pltpu
from jax.sharding import PartitionSpec as P

BF = jnp.bfloat16
F32 = jnp.float32
NX, NY, NZ = 8, 8, 4
NB, R, K = 1024, 1024, 256
H = 32
KC = 128
KY = 16
T = 256

NT = (((1,), (1,)), ((), ()))
NN = (((1,), (0,)), ((), ()))
MESH = pl.DeviceIdType.MESH
FAR = (4, 3, 5, 2, 6, 1, 7)


def kernel(
    ct_ref, vt_ref, f_ref, o_ref,
    vt, fac, part, cur, csend, crecv, ysend, yrecv, zsend, zrecv, zall, full, sc,
    fsem, vsem, xs, xr, zas, zar, zbs, zbr,
    cs, cr, ys, yr, zs, zr, zgs, zgr, ygs, ygr, cgs, cgr,
):
    rows, vecs = lax.axis_index("rows"), lax.axis_index("vecs")
    y, zh, c = rows // 8, (rows // 2) % 4, rows % 2
    x, zl = vecs // 2, vecs % 2

    def at(dx=0, dzl=0, dy=0, dz=0, dc=0):
        ry = (y + dy + NY) % NY
        rz = (zh + dz + NZ) % NZ
        rc = (c + dc) % 2
        vx = (x + dx + NX) % NX
        vz = (zl + dzl) % 2
        return (ry * 8 + rz * 2 + rc, vx * 2 + vz)

    def remote(src, dst, ssem, rsem, dev):
        return pltpu.make_async_remote_copy(
            src_ref=src, dst_ref=dst, send_sem=ssem, recv_sem=rsem, device_id=dev, device_id_type=MESH
        )

    barrier = pltpu.get_barrier_semaphore()
    peers = [at(dx=1), at(dx=-1), at(dzl=1), at(dc=1)]
    peers += [at(dy=d) for d in range(1, NY)] + [at(dz=d) for d in range(1, NZ)]
    for dev in peers:
        pl.semaphore_signal(barrier, inc=1, device_id=dev, device_id_type=MESH)

    copies = []
    fcopy = [pltpu.make_async_copy(f_ref.at[p], fac.at[p], fsem.at[p]) for p in (0, 1)]
    for p in (1, 0):
        fcopy[p].start()

    def blk(ox, ozl, h):
        return ((ox + NX) % NX * 2 + ozl) * 2 + h

    own = {}
    for p in (1, 0):
        for h in (0, 1):
            own[p, h] = pltpu.make_async_copy(vt_ref.at[p, h], vt.at[p, blk(x, zl, h)], vsem.at[p, h])
            own[p, h].start()

    pl.semaphore_wait(barrier, len(peers))

    sgn = 1 - 2 * c
    ITEM = ((0, 0), (0, 1), (1, 0))
    sends = []

    def slab(p, ox, item):
        oz, h = ITEM[item]
        return vt.at[p, blk(ox, (zl + oz) % 2, h)]

    def xcopy(p, item, direction, step):
        if step == 4:
            go, src = sgn, x - 3 * sgn
        elif direction == 0:
            go, src = 1, x - (step - 1)
        else:
            go, src = -1, x + (step - 1)
        source = slab(p, src, item)
        target = source
        if step == 1 and item < 2:
            source = vt_ref.at[p, ITEM[item][1]]
        return remote(source, target, xs.at[p, item, direction, step - 1], xr.at[p, item, direction, step - 1], at(dx=go))

    def xwait(p, item, direction, step):
        xcopy(p, item, direction, step).wait_recv()

    def zacopy(p):
        return remote(vt_ref.at[p, 0], vt.at[p, blk(x, zl, 0)], zas.at[p], zar.at[p], at(dzl=1))

    def zbcopy(p, n):
        ref = slab(p, x + n, 1)
        return remote(vt_ref.at[p, 1] if n == 0 else ref, ref, zbs.at[p, n], zbr.at[p, n], at(dzl=1))

    def begin(cp):
        cp.start()
        sends.append(cp)

    def gather0(p):
        begin(zacopy(p))
        for item in (0, 1):
            for d in (0, 1):
                begin(xcopy(p, item, d, 1))
        begin(zbcopy(p, 0))

    def gather1(p):
        zacopy(p).wait_recv()
        for d in (0, 1):
            begin(xcopy(p, 2, d, 1))

    def gather_step(p, s):
        for item in (0, 1, 2):
            if s == 4:
                xwait(p, item, 0, 4)
                if item == 1:
                    begin(zbcopy(p, 4))
                continue
            for d in (0, 1):
                xwait(p, item, d, s)
                if s < 3:
                    begin(xcopy(p, item, d, s + 1))
                if item == 1:
                    begin(zbcopy(p, (8 - s) if d == 0 else s))
            if s == 3:
                begin(xcopy(p, item, 0, 4))

    def gather_end(p):
        for n in range(NX):
            zbcopy(p, n).wait_recv()
        for h in (0, 1):
            own[p, h].wait()

    def partial(p, left):
        @pl.loop(0, NB // T)
        def _(i):
            v = vt[p, pl.ds(i * (T // H), T // H)].reshape(T, R)
            part[i] = lax.dot_general(left[...], v, NT, preferred_element_type=F32)

        oc = pl.multiple_of((1 - c) * KC, KC)
        for i in range(NB // T):
            csend[p, i] = part[i, pl.ds(oc, KC), :].astype(BF)

    def corecopy(p):
        return remote(csend.at[p], crecv.at[p], cs.at[p], cr.at[p], at(dc=1))

    def ycopy(p, d):
        return remote(ysend.at[p, (y + d) % NY], yrecv.at[p, d], ys.at[p, d], yr.at[p, d], at(dy=d))

    def zcopy(p, d):
        return remote(zsend.at[p, (zh + d) % NZ], zrecv.at[p, d], zs.at[p, d], zr.at[p, d], at(dz=d))

    def zgcopy(p, d):
        return remote(zall.at[p, zh], zall.at[p, zh], zgs.at[p, d], zgr.at[p, d], at(dz=d))

    def ygcopy(p, d):
        return remote(full.at[p, c, y], full.at[p, c, y], ygs.at[p, d], ygr.at[p, d], at(dy=d))

    def cgcopy(p, d):
        ref = full.at[p, c, (y - d + NY) % NY]
        return remote(ref, ref, cgs.at[p, d], cgr.at[p, d], at(dc=1))

    def reduce_y(p):
        corecopy(p).wait_recv()
        mine = pl.multiple_of(c * KC, KC)
        for i in range(NB // T):
            s = part[i, pl.ds(mine, KC), :] + crecv[p, i].astype(F32)
            part[i, 0:KC, :] = s
            ysend[p, :, :, i * T : (i + 1) * T] = s.astype(BF).reshape(NY, KY, T)
        for d in FAR:
            begin(ycopy(p, d))

    def reduce_z(p):
        tot = [part[i, pl.ds(pl.multiple_of(y * KY, KY), KY), :] for i in range(NZ)]
        for d in range(1, NY):
            ycopy(p, d).wait_recv()
        for d in range(1, NY):
            for i in range(NZ):
                tot[i] = tot[i] + yrecv[p, d, :, i * T : (i + 1) * T].astype(F32)
        for i in range(NZ):
            part[i, 0:KY, :] = tot[i]
            zsend[p, i] = tot[i].astype(BF)
        for d in (2, 1, 3):
            begin(zcopy(p, d))

    def gather_z(p):
        tot = part[zh, 0:KY, :]
        for d in range(1, NZ):
            zcopy(p, d).wait_recv()
        for d in range(1, NZ):
            tot = tot + zrecv[p, d].astype(F32)
        zall[p, zh] = tot.astype(BF)
        for d in (2, 1, 3):
            begin(zgcopy(p, d))

    def gather_y(p):
        for d in range(1, NZ):
            src = (zh - d + NZ) % NZ
            remote(zall.at[p, src], zall.at[p, src], zgs.at[p, d], zgr.at[p, d], at(dz=d)).wait_recv()
        for i in range(NZ):
            full[p, c, y, :, i * T : (i + 1) * T] = zall[p, i]
        for d in FAR:
            begin(ygcopy(p, d))
        begin(cgcopy(p, 0))

    def gather_core(p):
        for d in (1, 7, 2, 6, 3, 5, 4):
            src = (y - d + NY) % NY
            remote(full.at[p, c, src], full.at[p, c, src], ygs.at[p, d], ygr.at[p, d], at(dy=d)).wait_recv()
            begin(cgcopy(p, d))
        for d in range(NY):
            src = (y - d + NY) % NY
            remote(full.at[p, 1 - c, src], full.at[p, 1 - c, src], cgs.at[p, d], cgr.at[p, d], at(dc=1)).wait_recv()

    def apply(p, left, out):
        fcopy[p].wait()
        coeff = full.at[p]
        for i in range(NB // T):
            a = coeff[:, :, :, i * T :].reshape(K, NB - i * T)
            b = fac[p, i * T : (i + 1) * T, i * T :]
            sc[:, i * T : (i + 1) * T] = lax.dot_general(a, b, NT, preferred_element_type=F32).astype(BF)

        @pl.loop(0, R // T)
        def _(i):
            lanes = pl.ds(pl.multiple_of(i * T, T), T)
            v = vt[p, :, :, lanes].reshape(NB, T)
            upd = lax.dot_general(sc[...], v, NN, preferred_element_type=F32)
            out[:, lanes] = (left[:, lanes].astype(F32) - upd).astype(BF)

    gather0(1)
    gather1(1)
    for s in (1, 2, 3, 4):
        gather_step(1, s)
    gather0(0)
    gather_end(1)
    partial(1, ct_ref)
    begin(corecopy(1))
    gather1(0)
    reduce_y(1)
    gather_step(0, 1)
    reduce_z(1)
    gather_step(0, 2)
    gather_z(1)
    gather_step(0, 3)
    gather_y(1)
    gather_step(0, 4)
    gather_core(1)
    apply(1, ct_ref, cur)
    gather_end(0)
    partial(0, cur)
    begin(corecopy(0))
    reduce_y(0)
    reduce_z(0)
    gather_z(0)
    gather_y(0)
    gather_core(0)
    apply(0, cur, o_ref)
    for cp in sends:
        cp.wait_send()


def body(eigvecs, reflectors, factors):
    ct = eigvecs.T
    vt = jnp.swapaxes(reflectors, 1, 2).reshape(2, 2, H, R)
    dma = pltpu.SemaphoreType.DMA
    vmem = pl.BlockSpec(memory_space=pltpu.VMEM)
    out = pl.pallas_call(
        kernel,
        out_shape=jax.ShapeDtypeStruct((K, R), BF),
        in_specs=[vmem, vmem, pl.BlockSpec(memory_space=pl.ANY)],
        out_specs=vmem,
        scratch_shapes=[
            pltpu.VMEM((2, NB // H, H, R), BF),
            pltpu.VMEM((2, NB, NB), BF),
            pltpu.VMEM((NB // T, K, T), F32),
            pltpu.VMEM((K, R), BF),
            pltpu.VMEM((2, NB // T, KC, T), BF),
            pltpu.VMEM((2, NB // T, KC, T), BF),
            pltpu.VMEM((2, NY, KY, NB), BF),
            pltpu.VMEM((2, NY, KY, NB), BF),
            pltpu.VMEM((2, NZ, KY, T), BF),
            pltpu.VMEM((2, NZ, KY, T), BF),
            pltpu.VMEM((2, NZ, KY, T), BF),
            pltpu.VMEM((2, 2, NY, KY, NB), BF),
            pltpu.VMEM((K, NB), BF),
            dma((2,)), dma((2, 2)),
            dma((2, 3, 2, 4)), dma((2, 3, 2, 4)),
            dma((2,)), dma((2,)),
            dma((2, NX)), dma((2, NX)),
            dma((2,)), dma((2,)),
            dma((2, NY)), dma((2, NY)),
            dma((2, NZ)), dma((2, NZ)),
            dma((2, NZ)), dma((2, NZ)),
            dma((2, NY)), dma((2, NY)),
            dma((2, NY)), dma((2, NY)),
        ],
        compiler_params=pltpu.CompilerParams(
            collective_id=0, has_side_effects=True, vmem_limit_bytes=40 * 1024 * 1024
        ),
        name="reflect",
    )(ct, vt, factors)
    return out.T


def solution(mesh):
    in_specs = (P("rows", "vecs"), P(None, "rows", "vecs"), P())
    out_specs = P("rows", "vecs")
    return jax.shard_map(body, mesh=mesh, in_specs=in_specs, out_specs=out_specs, check_vma=False)
```

time: 695 us -> 110 us (0.16); the launches traced: 686 us -> 110 us
  blocking collectives: 575 us -> 0 us
  Pallas kernels: 0 us -> 105 us
  waiting for transfers between devices: 80.7 us -> 0 us
  between operations: 13.4 us -> 0.02 us
  matrix products: 12.5 us -> 0 us
    psum x2 -> x0, blocking collectives: 575 us -> none  [body(): coeff = lax.psum(partial_value, 'rows').astype(jnp.bfloat16)]
    pallas_call x0 -> x1, Pallas kernels: none -> 105 us  [body(): pl.pallas_call(kernel, out_shape=jax.ShapeDtypeStruct((K, R), BF), in_spe...]
    all_gather x2 -> x0, waiting for transfers between devices: 80 us -> none  [body(): panel = lax.all_gather(reflectors[which], 'vecs', axis=1, tiled=True)]
    dot_general x4 -> x0, matrix products: 12.5 us -> none  [the longest x2 7.43 us: body(): update = jnp.dot(panel, scaled, preferred_element_type=jnp.float32)]
  transfers between devices with their start and end apart: 2 -> 0, of which waited for: 1 -> 0; matrix products, arithmetic and copies ran while one was open for 1% -> 0% of each run, Pallas kernels for 0% -> 0%
where the time goes in v1:
time: 110 us
  Pallas kernels  105 us (95%)
  local copies, waits for them, and re-layouts  5.38 us (5%)
    pallas_call x1, Pallas kernels, body(): pl.pallas_call(kernel, out_shape=jax.ShapeDtypeStruct((K, R), BF), in_spe...  105 us
    unnamed x5, local copies, waits for them, and re-layouts  4.38 us

profile of v1, /device:TPU:1, one launch (start us, length us, event | category | flops | bytes accessed | tf_op | source)
XLA Modules:
  0.0 110.0 jit_solution(18329410239805603187)
XLA Ops:
  0.0 1.2 %copy.4 = bf16[1024,256]{0,1:T(8,128)(2,1)S(1)} copy(bf16[1024,256]{1,0:T(8,128)(2,1)} %param.3) | data formatting | bytes 1048576 | tf_op args[0]
  1.3 0.0 copy-start
  1.3 2.2 %copy-done = bf16[2,1024,1024]{2,1,0:T(8,128)(2,1)S(1)} copy-done((bf16[2,1024,1024]{2,1,0:T(8,128)(2,1)S(1)}, bf16[2,1024,1024]{2,1,0:T(8,128)(2,1)}, u32[]{:S(2)}) %copy-start) | copy-done | bytes 4194328
  3.4 0.0 copy-start.1
  3.4 0.9 copy-done.1
  4.4 104.6 %reflect.1 = bf16[256,1024]{1,0:T(8,128)(2,1)S(1)} custom-call(bf16[256,1024]{1,0:T(8,128)(2,1)S(1)} %bitcast.6, bf16[2,2,32,1024]{3,2,1,0:T(8,128)(2,1)S(1)} %bitcast.7, bf16[2,1024,1024]{2,1,0:T(8,128)(2,1)S(1)} %copy-done), custom_call_target="tpu_custom_call" | custom-call | tf_op jit(solution)/shard_map/reflect/pallas_call | solution.py:270
  109.0 1.0 copy.5
Async XLA Ops:
  1.3 2.2 %copy-start = (bf16[2,1024,1024]{2,1,0:T(8,128)(2,1)S(1)}, bf16[2,1024,1024]{2,1,0:T(8,128)(2,1)}, u32[]{:S(2)}) copy-start(bf16[2,1024,1024]{2,1,0:T(8,128)(2,1)} %f_ref.1) | copy-start | bytes 12582916
  3.4 0.9 copy-start.1

commit v2 on v0

v2 whole, which is shorter than its diff:
```python
import jax
import jax.numpy as jnp
from jax import lax
from jax.experimental import pallas as pl
from jax.experimental.pallas import tpu as pltpu
from jax.sharding import PartitionSpec as P

BF = jnp.bfloat16
F32 = jnp.float32
NX, NY, NZ = 8, 8, 4
NB, R, K = 1024, 1024, 256
H = 32
KC = 128
KY = 16
T = 256

NT = (((1,), (1,)), ((), ()))
NN = (((1,), (0,)), ((), ()))
MESH = pl.DeviceIdType.MESH
PLANE = sorted(
    [(a, b) for a in range(NY) for b in range(NZ) if a or b],
    key=lambda d: (-min(d[0], NY - d[0]) - 2 * min(d[1], NZ - d[1]), d),
)


def kernel(
    e_ref, vt_ref, f_ref, o_ref,
    vt, fac, nat, ct, part, half, cur, csend, crecv, rsend, rrecv, full, sc,
    esem, fsem, osem, ssem, zsem, zbsem, x1sem, x0sem, csem, rsem, gsem, hsem,
):
    rows, vecs = lax.axis_index("rows"), lax.axis_index("vecs")
    y, zh, c = rows // 8, (rows // 2) % 4, rows % 2
    x, zl = vecs // 2, vecs % 2

    def at(dx=0, dzl=0, dy=0, dz=0, dc=0):
        ry = (y + dy) % NY
        rz = (zh + dz) % NZ
        rc = (c + dc) % 2
        vx = (x + dx + NX) % NX
        vz = (zl + dzl) % 2
        return (ry * 8 + rz * 2 + rc, vx * 2 + vz)

    def remote(src, dst, send, recv, dev):
        return pltpu.make_async_remote_copy(
            src_ref=src, dst_ref=dst, send_sem=send, recv_sem=recv, device_id=dev, device_id_type=MESH
        )

    with jax.named_scope("S_pre"):
        barrier = pltpu.get_barrier_semaphore()
        peers = [at(dx=1), at(dx=-1), at(dzl=1), at(dc=1)] + [at(dy=a, dz=b) for a, b in PLANE]
        for dev in peers:
            pl.semaphore_signal(barrier, inc=1, device_id=dev, device_id_type=MESH)

        def blk(ox, ozl, h=0):
            return ((ox + NX) % NX * 2 + ozl) * 2 + h

        ecopy = pltpu.make_async_copy(e_ref, nat, esem)
        ecopy.start()
        own = [pltpu.make_async_copy(vt_ref.at[p], vt.at[p, pl.ds(blk(x, zl), 2)], osem.at[p]) for p in (0, 1)]
        fcopy = [pltpu.make_async_copy(f_ref.at[p], fac.at[p], fsem.at[p]) for p in (0, 1)]
        for p in (1, 0):
            own[p].start()
            fcopy[p].start()

    with jax.named_scope("S_barrier"):
        pl.semaphore_wait(barrier, len(peers))

    sgn = 1 - 2 * c

    A, B, O = 0, 1, 2
    ITEM = ((0, 0), (0, 1), (1, 0))
    GROUP = {0: 0, 1: 1, 7: 1, 2: 2, 6: 2, 3: 3, 5: 3, 4: 4}

    def hop(step, direction):
        if step == 4:
            return sgn, x - 3 * sgn
        return (1, x - (step - 1)) if direction == 0 else (-1, x + (step - 1))

    def x1(item, direction, step):
        go, src = hop(step, direction)
        oz, h = ITEM[item]
        target = vt.at[1, blk(src, (zl + oz) % 2, h)]
        source = vt_ref.at[1, h] if step == 1 and item != O else target
        return remote(source, target, ssem.at[1], x1sem.at[item, direction, step - 1], at(dx=go))

    def za1():
        return remote(vt_ref.at[1, 0], vt.at[1, blk(x, zl, 0)], ssem.at[1], zsem.at[1], at(dzl=1))

    def zb1(n):
        ref = vt.at[1, blk(x + n, zl, 1)]
        return remote(vt_ref.at[1, 1] if n == 0 else ref, ref, ssem.at[1], zbsem.at[GROUP[n]], at(dzl=1))

    def start1(item, step):
        for d in (0,) if step == 4 else (0, 1):
            x1(item, d, step).start()

    def pass1(item, step):
        for d in (0,) if step == 4 else (0, 1):
            x1(item, d, step).wait_recv()
            if step < 3:
                x1(item, d, step + 1).start()
        if step == 3:
            x1(item, 0, 4).start()
        if item == B:
            for n in (4,) if step == 4 else (8 - step, step):
                zb1(n).start()

    def zb1_wait(g):
        k = 1 if g in (0, 4) else 2
        ref = vt.at[1, pl.ds(0, k)]
        remote(ref, ref, ssem.at[1], zbsem.at[g], at(dzl=1)).wait_recv()

    def x0(item, direction, step):
        go, src = hop(step, direction)
        target = vt.at[0, pl.ds(blk(src, (zl + item) % 2), 2)]
        source = vt_ref.at[0] if step == 1 and item == 0 else target
        return remote(source, target, ssem.at[0], x0sem.at[item, direction, step - 1], at(dx=go))

    def z0():
        return remote(vt_ref.at[0], vt.at[0, pl.ds(blk(x, zl), 2)], ssem.at[0], zsem.at[0], at(dzl=1))

    def start0(item):
        for d in (0, 1):
            x0(item, d, 1).start()

    def pass0(item, step):
        for d in (0,) if step == 4 else (0, 1):
            x0(item, d, step).wait_recv()
            if step < 3:
                x0(item, d, step + 1).start()
        if step == 3:
            x0(item, 0, 4).start()

    def partial(p, left, i):
        v = vt[p, pl.ds(i * (T // H), T // H)].reshape(T, R)
        part[i] = lax.dot_general(left[...], v, NT, preferred_element_type=F32)
        oc = pl.multiple_of((1 - c) * KC, KC)
        csend[p, i] = part[i, pl.ds(oc, KC), :].astype(BF)

    def corecopy(p, i, n):
        return remote(csend.at[p, i], crecv.at[p, i], ssem.at[2 + p], csem.at[p, n], at(dc=1))

    def add_core(p, i, n):
        corecopy(p, i, n).wait_recv()
        mine = pl.multiple_of(c * KC, KC)
        s = part[i, pl.ds(mine, KC), :] + crecv[p, i].astype(F32)
        half[i] = s
        rsend[p, i] = s.astype(BF).reshape(NY, KY, T)

    def scatter(p):
        for n, (a, b) in enumerate(PLANE):
            src = rsend.at[p, (zh + b) % NZ, (y + a) % NY]
            remote(src, rrecv.at[p, n], ssem.at[4 + p], rsem.at[p], at(dy=a, dz=b)).start()

    def reduce(p):
        tot = half[zh, pl.ds(pl.multiple_of(y * KY, KY), KY), :]
        ref = rrecv.at[p]
        remote(ref, ref, ssem.at[4 + p], rsem.at[p], at(dy=1)).wait_recv()
        for n in range(len(PLANE)):
            tot = tot + rrecv[p, n].astype(F32)
        full[p, c, zh, y] = tot.astype(BF)
        ref = full.at[p, c, zh, y]
        for a, b in PLANE:
            remote(ref, ref, ssem.at[6 + p], gsem.at[p, (NZ - b) % NZ], at(dy=a, dz=b)).start()

    def spread(p, b):
        ref = full.at[p, c, (zh + b) % NZ]
        got = ref if b else full.at[p, c, zh, pl.ds(0, NY - 1)]
        remote(got, got, ssem.at[6 + p], gsem.at[p, b], at(dy=1)).wait_recv()
        remote(ref, ref, ssem.at[8 + p], hsem.at[p], at(dc=1)).start()

    def spread_end(p):
        ref = full.at[p, 1 - c]
        remote(ref, ref, ssem.at[8 + p], hsem.at[p], at(dc=1)).wait_recv()

    def apply(p, left):
        fcopy[p].wait()
        for i in range(NB // T):
            acc = None
            for j in range(i, NB // T):
                a = full[p, :, j].reshape(K, T)
                b = fac[p, i * T : (i + 1) * T, j * T : (j + 1) * T]
                t = lax.dot_general(a, b, NT, preferred_element_type=F32)
                acc = t if acc is None else acc + t
            sc[:, i * T : (i + 1) * T] = acc.astype(BF)

        @pl.loop(0, R // T)
        def _(i):
            lanes = pl.ds(pl.multiple_of(i * T, T), T)
            v = vt[p, :, :, lanes].reshape(NB, T)
            upd = lax.dot_general(sc[...], v, NN, preferred_element_type=F32)
            new = (left[:, lanes].astype(F32) - upd).astype(BF)
            if p == 1:
                cur[:, lanes] = new
            else:
                o_ref[lanes, :] = new.T

    scope = jax.named_scope
    e = 1 - 2 * (x % 2)
    tiles = [(x // 2 + d + NZ) % NZ for d in (0, -e, e, 2)]

    def tile1(n):
        partial(1, ct, tiles[n])
        corecopy(1, tiles[n], n).start()
        if n > 0:
            add_core(1, tiles[n - 1], n - 1)

    with scope("S00_start"):
        za1().start()
        start1(B, 1)
        start1(A, 1)
        zb1(0).start()
    with scope("S01_transpose"):
        ecopy.wait()
        for i in range(R // T):
            ct[:, i * T : (i + 1) * T] = nat[i * T : (i + 1) * T, :].T
    with scope("S02_z"):
        za1().wait_recv()
        start1(O, 1)
    with scope("S03_BA1"):
        pass1(B, 1)
        pass1(A, 1)
    with scope("S04_OBA2"):
        pass1(O, 1)
        pass1(B, 2)
        pass1(A, 2)
    with scope("S05_tile0"):
        own[1].wait()
        zb1_wait(0)
        zb1_wait(1)
        tile1(0)
    with scope("S06_OBA3"):
        pass1(O, 2)
        pass1(B, 3)
        pass1(A, 3)
    with scope("S07_tile1"):
        zb1_wait(2)
        tile1(1)
    with scope("S08_O3"):
        pass1(O, 3)
        z0().start()
        start0(0)
    with scope("S09_BA4"):
        pass1(B, 4)
        pass1(A, 4)
    with scope("S10_tile2"):
        zb1_wait(3)
        tile1(2)
    with scope("S11_O4"):
        pass1(O, 4)
        zb1_wait(4)
    with scope("S12_tile3"):
        tile1(3)
        add_core(1, tiles[3], 3)
    with scope("S13_scatter"):
        scatter(1)
    with scope("S14_v0"):
        z0().wait_recv()
        start0(1)
        pass0(0, 1)
        pass0(1, 1)
        pass0(0, 2)
    with scope("S15_reduce"):
        reduce(1)
    with scope("S16_v0"):
        pass0(1, 2)
        pass0(0, 3)
    with scope("S17_spread"):
        spread(1, 0)
    with scope("S18_v0"):
        pass0(1, 3)
    with scope("S19_spread"):
        spread(1, 1)
        spread(1, 3)
        spread(1, 2)
        spread_end(1)
    with scope("S22_apply"):
        apply(1, ct)
    with scope("S23_v0"):
        pass0(0, 4)
        pass0(1, 4)
        own[0].wait()
    with scope("S24_partial"):
        for i in range(NZ):
            partial(0, cur, i)
            corecopy(0, i, i).start()
    with scope("S25_core"):
        for i in range(NZ):
            add_core(0, i, i)
    with scope("S26_scatter"):
        scatter(0)
    with scope("S27_reduce"):
        reduce(0)
    with scope("S28_spread"):
        for b in (0, 1, 3, 2):
            spread(0, b)
        spread_end(0)
    with scope("S29_apply"):
        apply(0, cur)
    with scope("S99_drain"):
        for p in (0, 1):
            sent = [vt.at[p, pl.ds(0, 30)], csend.at[p], rrecv.at[p], rrecv.at[p], full.at[p, c]]
            for k, ref in enumerate(sent):
                remote(ref, ref, ssem.at[2 * k + p], hsem.at[p], at(dc=1)).wait_send()


def body(eigvecs, reflectors, factors):
    vt = jnp.swapaxes(reflectors, 1, 2).reshape(2, 2, H, R)
    dma = pltpu.SemaphoreType.DMA
    hbm = pl.BlockSpec(memory_space=pltpu.HBM)
    n = len(PLANE)
    out = pl.pallas_call(
        kernel,
        out_shape=jax.ShapeDtypeStruct((R, K), BF),
        in_specs=[hbm, hbm, hbm],
        out_specs=pl.BlockSpec(memory_space=pltpu.VMEM),
        scratch_shapes=[
            pltpu.VMEM((2, NB // H, H, R), BF),
            pltpu.VMEM((2, NB, NB), BF),
            pltpu.VMEM((R, K), BF),
            pltpu.VMEM((K, R), BF),
            pltpu.VMEM((NZ, K, T), F32),
            pltpu.VMEM((NZ, KC, T), F32),
            pltpu.VMEM((K, R), BF),
            pltpu.VMEM((2, NZ, KC, T), BF),
            pltpu.VMEM((2, NZ, KC, T), BF),
            pltpu.VMEM((2, NZ, NY, KY, T), BF),
            pltpu.VMEM((2, n, KY, T), BF),
            pltpu.VMEM((2, 2, NZ, NY, KY, T), BF),
            pltpu.VMEM((K, NB), BF),
            dma(()), dma((2,)), dma((2,)),
            dma((10,)),
            dma((2,)), dma((5,)),
            dma((3, 2, 4)), dma((2, 2, 4)),
            dma((2, NZ)), dma((2,)), dma((2, NZ)), dma((2,)),
        ],
        compiler_params=pltpu.CompilerParams(
            collective_id=0, has_side_effects=True, vmem_limit_bytes=60 * 1024 * 1024
        ),
        name="reflect",
    )(eigvecs, vt, factors)
    return out


def solution(mesh):
    in_specs = (P("rows", "vecs"), P(None, "rows", "vecs"), P())
    out_specs = P("rows", "vecs")
    return jax.shard_map(body, mesh=mesh, in_specs=in_specs, out_specs=out_specs, check_vma=False)
```

time: 695 us -> 97.5 us (0.14); the launches traced: 686 us -> 97.3 us
  blocking collectives: 575 us -> 0 us
  Pallas kernels: 0 us -> 95.5 us
  waiting for transfers between devices: 80.7 us -> 0 us
  between operations: 13.4 us -> 0.01 us
  matrix products: 12.5 us -> 0 us
    psum x2 -> x0, blocking collectives: 575 us -> none  [body(): coeff = lax.psum(partial_value, 'rows').astype(jnp.bfloat16)]
    pallas_call x0 -> x1, Pallas kernels: none -> 95.5 us  [body(): pl.pallas_call(kernel, out_shape=jax.ShapeDtypeStruct((R, K), BF), in_spe...]
    all_gather x2 -> x0, waiting for transfers between devices: 80 us -> none  [body(): panel = lax.all_gather(reflectors[which], 'vecs', axis=1, tiled=True)]
    dot_general x4 -> x0, matrix products: 12.5 us -> none  [the longest x2 7.43 us: body(): update = jnp.dot(panel, scaled, preferred_element_type=jnp.float32)]
  transfers between devices with their start and end apart: 2 -> 0, of which waited for: 1 -> 0; matrix products, arithmetic and copies ran while one was open for 1% -> 0% of each run, Pallas kernels for 0% -> 0%
where the time goes in v2:
time: 97.5 us; the launch traced here: 97.3 us
  Pallas kernels  95.5 us (98%)
  local copies, waits for them, and re-layouts  1.87 us (2%)
    pallas_call x1, Pallas kernels, body(): pl.pallas_call(kernel, out_shape=jax.ShapeDtypeStruct((R, K), BF), in_spe...  95.5 us

profile of v2, /device:TPU:1, one launch (start us, length us, event | category | flops | bytes accessed | tf_op | source)
XLA Modules:
  0.0 97.3 jit_solution(976343042505039931)
XLA Ops:
  0.0 95.5 %reflect.1 = bf16[1024,256]{1,0:T(8,128)(2,1)} custom-call(bf16[1024,256]{1,0:T(8,128)(2,1)} %e_ref.1, bf16[2,2,32,1024]{3,2,1,0:T(8,128)(2,1)} %bitcast.3, bf16[2,1024,1024]{2,1,0:T(8,128)(2,1)} %f_ref.1), custom_call_target="tpu_custom_call" | custom-call | tf_op jit(solution)/shard_map/reflect/pallas_call | solution.py:312
  95.5 1.9 %copy.5 = bf16[1024,256]{1,0:T(8,128)(2,1)} copy(bf16[1024,256]{1,0:T(8,128)(2,1)} %reflect.1) | data formatting | bytes 1048576

commit v3 on v0

v3 whole, which is shorter than its diff:
```python
import jax
import jax.numpy as jnp
from jax import lax
from jax.experimental import pallas as pl
from jax.experimental.pallas import tpu as pltpu
from jax.sharding import PartitionSpec as P

BF = jnp.bfloat16
F32 = jnp.float32
NX, NY, NZ = 8, 8, 4
NB, R, K = 1024, 1024, 256
H = 16
U = 4
FIRST = (3, 2)
SENT = [(1 + 14) * n + (7 + 8) * (U - n) for n in FIRST]
KH = 128
KC = 64
KY = 16
T = 256
TL = 128

NT = (((1,), (1,)), ((), ()))
NN = (((1,), (0,)), ((), ()))
MESH = pl.DeviceIdType.MESH
PLANE = sorted(
    [(a, b) for a in range(NY) for b in range(NZ) if a or b],
    key=lambda d: (-min(d[0], NY - d[0]) - 2 * min(d[1], NZ - d[1]), d),
)


def kernel(
    e_ref, vt_ref, f_ref, o_ref,
    vt, fac, nat, ct, part, half, cur, csend, crecv, rsend, rrecv, full, sc,
    esem, fsem, osem, ssem, zsem, zbsem, xsem, csem, rsem, gsem, hsem, in_z, in_y,
):
    rows, vecs = lax.axis_index("rows"), lax.axis_index("vecs")
    y, zh, c = rows // 8, (rows // 2) % 4, rows % 2
    x, zl = vecs // 2, vecs % 2

    def at(dx=0, dzl=0, dy=0, dz=0, dc=0):
        ry = (y + dy) % NY
        rz = (zh + dz) % NZ
        rc = (c + dc) % 2
        vx = (x + dx + NX) % NX
        vz = (zl + dzl) % 2
        return (ry * 8 + rz * 2 + rc, vx * 2 + vz)

    def remote(src, dst, send, recv, dev):
        return pltpu.make_async_remote_copy(
            src_ref=src, dst_ref=dst, send_sem=send, recv_sem=recv, device_id=dev, device_id_type=MESH
        )

    with jax.named_scope("S_pre"):
        barrier = pltpu.get_barrier_semaphore()
        peers = [at(dx=1), at(dx=-1), at(dzl=1), at(dc=1), at(dy=1), at(dy=-1), at(dz=1), at(dz=-1)]
        for dev in peers:
            pl.semaphore_signal(barrier, inc=1, device_id=dev, device_id_type=MESH)

        def blk(ox, ozl):
            return ((ox + NX) % NX * 2 + ozl) * U

        ecopy = pltpu.make_async_copy(e_ref, nat, esem)
        ecopy.start()
        own = [pltpu.make_async_copy(vt_ref.at[p], vt.at[p, pl.ds(blk(x, zl), U)], osem.at[p]) for p in (0, 1)]
        fcopy = [pltpu.make_async_copy(f_ref.at[p], fac.at[p], fsem.at[p]) for p in (0, 1)]
        for p in (1, 0):
            own[p].start()
            fcopy[p].start()

    with jax.named_scope("S_barrier"):
        pl.semaphore_wait(barrier, len(peers))

    def tell(sem, dev):
        pl.semaphore_signal(sem, inc=1, device_id=dev, device_id_type=MESH)

    def hear(n):
        if n == 0:
            tell(in_z, at(dz=-1))
            return
        if n == 1:
            pl.semaphore_wait(in_z, 1)
        else:
            for d in (0, 1):
                pl.semaphore_wait(in_y.at[n - 2, d], 1)
        if n <= NY // 2:
            tell(in_y.at[n - 1, 0], at(dy=1))
            tell(in_y.at[n - 1, 1], at(dy=-1))

    sgn = 1 - 2 * c

    A, B, O = 0, 1, 2
    GROUP = {0: 0, 1: 1, 7: 1, 2: 2, 6: 2, 3: 3, 5: 3, 4: 4}

    def units(p, item):
        return (FIRST[p], U - FIRST[p]) if item == B else (0, FIRST[p])

    def hop(step, direction):
        if step == 4:
            return sgn, x - 3 * sgn
        return (1, x - (step - 1)) if direction == 0 else (-1, x + (step - 1))

    def xcopy(p, item, direction, step):
        go, src = hop(step, direction)
        at_unit, n = units(p, item)
        target = vt.at[p, pl.ds(blk(src, (zl + (item == O)) % 2) + at_unit, n)]
        source = vt_ref.at[p, at_unit : at_unit + n] if step == 1 and item != O else target
        return remote(source, target, ssem.at[p], xsem.at[p, item, direction, step - 1], at(dx=go))

    def za(p):
        return remote(vt_ref.at[p, : FIRST[p]], vt.at[p, pl.ds(blk(x, zl), FIRST[p])], ssem.at[p], zsem.at[p], at(dzl=1))

    def zbsem_of(p, g):
        return zbsem.at[g if p == 1 else 5]

    def zb(p, k):
        at_unit, n = units(p, B)
        ref = vt.at[p, pl.ds(blk(x + k, zl) + at_unit, n)]
        return remote(vt_ref.at[p, at_unit:] if k == 0 else ref, ref, ssem.at[p], zbsem_of(p, GROUP[k]), at(dzl=1))

    def start(p, item):
        for d in (0, 1):
            xcopy(p, item, d, 1).start()

    def forward(p, item, step):
        for d in (0,) if step == 4 else (0, 1):
            xcopy(p, item, d, step).wait_recv()
            if step < 3:
                xcopy(p, item, d, step + 1).start()
        if step == 3:
            xcopy(p, item, 0, 4).start()
        if item == B:
            for k in (4,) if step == 4 else (8 - step, step):
                zb(p, k).start()

    def zb_wait(p, g, blocks):
        ref = vt.at[p, pl.ds(0, blocks * (U - FIRST[p]))]
        remote(ref, ref, ssem.at[p], zbsem_of(p, g), at(dzl=1)).wait_recv()

    def mine(hf, who):
        return pl.ds(pl.multiple_of(hf * KH + who * KC, KC), KC)

    def partial(p, left, i):
        v = vt[p, pl.ds(i * (T // H), T // H)].reshape(T, R)
        part[i] = lax.dot_general(left[...], v, NT, preferred_element_type=F32)

    def outgoing(p, i, hf):
        csend[p, i, hf] = part[i, mine(hf, 1 - c), :].astype(BF)

    def core1(i, n):
        return remote(csend.at[1, i], crecv.at[1, i], ssem.at[3], csem.at[n], at(dc=1))

    def core0(i, hf):
        return remote(csend.at[0, i, hf], crecv.at[0, i, hf], ssem.at[2], csem.at[NZ + hf], at(dc=1))

    def add_core(p, i, hf):
        s = part[i, mine(hf, c), :] + crecv[p, i, hf].astype(F32)
        for q in (0, 1):
            t = s[:, q * TL : (q + 1) * TL].reshape(NY // 2, KY, TL)
            half[hf, i, q * (NY // 2) : (q + 1) * (NY // 2)] = t
            rsend[p, hf, i, q * (NY // 2) : (q + 1) * (NY // 2)] = t.astype(BF)

    def scatter(p, hf):
        for n, (a, b) in enumerate(PLANE):
            src = rsend.at[p, hf, (zh + b) % NZ, (y + a) % NY]
            remote(src, rrecv.at[p, hf, n], ssem.at[4 + 2 * p + hf], rsem.at[p, hf], at(dy=a, dz=b)).start()

    def reduce(p, hf):
        tot = half[hf, zh, y]
        ref = rrecv.at[p, hf]
        remote(ref, ref, ssem.at[4 + 2 * p + hf], rsem.at[p, hf], at(dy=1)).wait_recv()
        for n in range(len(PLANE)):
            tot = tot + rrecv[p, hf, n].astype(F32)
        full[p, hf, c, zh, y] = tot.astype(BF)
        ref = full.at[p, hf, c, zh, y]
        for a, b in PLANE:
            remote(ref, ref, ssem.at[8 + 2 * p + hf], gsem.at[p, hf, (NZ - b) % NZ], at(dy=a, dz=b)).start()

    def spread(p, hf):
        for b in (0, 1, 3, 2):
            ref = full.at[p, hf, c, (zh + b) % NZ]
            got = ref if b else full.at[p, hf, c, zh, pl.ds(0, NY - 1)]
            remote(got, got, ssem.at[8 + 2 * p + hf], gsem.at[p, hf, b], at(dy=1)).wait_recv()
            remote(ref, ref, ssem.at[12 + 2 * p + hf], hsem.at[p, hf], at(dc=1)).start()

    def spread_end(p, hf):
        ref = full.at[p, hf, 1 - c]
        remote(ref, ref, ssem.at[12 + 2 * p + hf], hsem.at[p, hf], at(dc=1)).wait_recv()

    def apply(p, left):
        fcopy[p].wait()
        coeff = []
        for j in range(NZ):
            w = full[p, :, :, j]
            coeff.append(jnp.concatenate([w[:, :, : NY // 2].reshape(K, TL), w[:, :, NY // 2 :].reshape(K, TL)], axis=1))
        for i in range(NB // T):
            acc = None
            for j in range(i, NB // T):
                b = fac[p, i * T : (i + 1) * T, j * T : (j + 1) * T]
                t = lax.dot_general(coeff[j], b, NT, preferred_element_type=F32)
                acc = t if acc is None else acc + t
            sc[:, i * T : (i + 1) * T] = acc.astype(BF)

        @pl.loop(0, R // T)
        def _(i):
            lanes = pl.ds(pl.multiple_of(i * T, T), T)
            v = vt[p, :, :, lanes].reshape(NB, T)
            upd = lax.dot_general(sc[...], v, NN, preferred_element_type=F32)
            new = (left[:, lanes].astype(F32) - upd).astype(BF)
            if p == 1:
                cur[:, lanes] = new
            else:
                o_ref[lanes, :] = new.T

    scope = jax.named_scope
    e = 1 - 2 * (x % 2)
    tiles = [(x // 2 + d + NZ) % NZ for d in (0, -e, e, 2)]

    def add1(n):
        core1(tiles[n], n).wait_recv()
        for hf in (0, 1):
            add_core(1, tiles[n], hf)

    def tile1(n):
        partial(1, ct, tiles[n])
        for hf in (0, 1):
            outgoing(1, tiles[n], hf)
        core1(tiles[n], n).start()
        if n > 0:
            add1(n - 1)

    def partial0():
        @pl.loop(0, NZ)
        def _(i):
            partial(0, cur, i)

        for hf in (0, 1):
            for i in range(NZ):
                outgoing(0, i, hf)
                core0(i, hf).start()

    def add0(hf):
        ref = crecv.at[0, pl.ds(0, 2)]
        remote(ref, ref, ssem.at[2], csem.at[NZ + hf], at(dc=1)).wait_recv()
        for i in range(NZ):
            add_core(0, i, hf)

    with scope("S00_start"):
        za(1).start()
        start(1, B)
        start(1, A)
        zb(1, 0).start()
        hear(0)
    with scope("S01_transpose"):
        ecopy.wait()
        for i in range(R // T):
            ct[:, i * T : (i + 1) * T] = nat[i * T : (i + 1) * T, :].T
    with scope("S02_z"):
        za(1).wait_recv()
        start(1, O)
    with scope("S03_BA1"):
        forward(1, B, 1)
        forward(1, A, 1)
        hear(1)
    with scope("S04_OBA2"):
        forward(1, O, 1)
        forward(1, B, 2)
        forward(1, A, 2)
        hear(2)
    with scope("S05_tile0"):
        own[1].wait()
        zb_wait(1, 0, 1)
        zb_wait(1, 1, 2)
        tile1(0)
    with scope("S06_OBA3"):
        forward(1, O, 2)
        forward(1, B, 3)
        forward(1, A, 3)
        hear(3)
    with scope("S07_tile1"):
        zb_wait(1, 2, 2)
        tile1(1)
    with scope("S08_O3"):
        forward(1, O, 3)
    with scope("S09_BA4"):
        forward(1, B, 4)
        za(0).start()
        forward(1, A, 4)
        hear(4)
    with scope("S10_tile2"):
        zb_wait(1, 3, 2)
        tile1(2)
    with scope("S11_O4"):
        forward(1, O, 4)
        start(0, B)
        start(0, A)
        zb(0, 0).start()
        zb_wait(1, 4, 1)
    with scope("S12_tile3"):
        tile1(3)
        add1(3)
    with scope("S13_scatter"):
        hear(5)
        scatter(1, 0)
        scatter(1, 1)
    with scope("S14_v0"):
        za(0).wait_recv()
        start(0, O)
        forward(0, B, 1)
        forward(0, A, 1)
        forward(0, O, 1)
    with scope("S15_reduceA"):
        reduce(1, 0)
    with scope("S16_v0"):
        forward(0, B, 2)
        forward(0, A, 2)
    with scope("S17_reduceB"):
        reduce(1, 1)
    with scope("S18_v0"):
        forward(0, O, 2)
        forward(0, B, 3)
        forward(0, A, 3)
    with scope("S19_spreadA"):
        spread(1, 0)
    with scope("S20_v0"):
        forward(0, O, 3)
    with scope("S21_spreadB"):
        spread(1, 1)
    with scope("S22_v0"):
        forward(0, B, 4)
    with scope("S23_spreadend"):
        spread_end(1, 0)
        spread_end(1, 1)
    with scope("S24_apply"):
        apply(1, ct)
    with scope("S25_v0"):
        forward(0, A, 4)
        forward(0, O, 4)
        zb_wait(0, 5, NX)
        own[0].wait()
    with scope("S26_partial"):
        partial0()
    with scope("S27_scatter"):
        for hf in (0, 1):
            add0(hf)
            scatter(0, hf)
    with scope("S30_reduceA"):
        reduce(0, 0)
    with scope("S31_reduceB"):
        reduce(0, 1)
    with scope("S32_spreadA"):
        spread(0, 0)
    with scope("S33_spreadB"):
        spread(0, 1)
    with scope("S34_spreadend"):
        spread_end(0, 0)
        spread_end(0, 1)
    with scope("S35_apply"):
        apply(0, cur)
    with scope("S99_drain"):
        sent = [(1, vt.at[1, pl.ds(0, SENT[1])]), (0, vt.at[0, pl.ds(0, SENT[0])])] + [(2 + p, csend.at[p]) for p in (0, 1)]
        for p in (0, 1):
            for hf in (0, 1):
                m = 2 * p + hf
                sent += [(4 + m, rrecv.at[p, hf]), (8 + m, rrecv.at[p, hf]), (12 + m, full.at[p, hf, c])]
        for m, ref in sent:
            remote(ref, ref, ssem.at[m], hsem.at[0, 0], at(dc=1)).wait_send()


def body(eigvecs, reflectors, factors):
    vt = jnp.swapaxes(reflectors, 1, 2).reshape(2, U, H, R)
    dma = pltpu.SemaphoreType.DMA
    hbm = pl.BlockSpec(memory_space=pltpu.HBM)
    n = len(PLANE)
    out = pl.pallas_call(
        kernel,
        out_shape=pltpu.VMEM((R, K), BF),
        in_specs=[hbm, hbm, hbm],
        out_specs=pl.BlockSpec(memory_space=pltpu.VMEM),
        scratch_shapes=[
            pltpu.VMEM((2, NB // H, H, R), BF),
            pltpu.VMEM((2, NB, NB), BF),
            pltpu.VMEM((R, K), BF),
            pltpu.VMEM((K, R), BF),
            pltpu.VMEM((NZ, K, T), F32),
            pltpu.VMEM((2, NZ, NY, KY, TL), F32),
            pltpu.VMEM((K, R), BF),
            pltpu.VMEM((2, NZ, 2, KC, T), BF),
            pltpu.VMEM((2, NZ, 2, KC, T), BF),
            pltpu.VMEM((2, 2, NZ, NY, KY, TL), BF),
            pltpu.VMEM((2, 2, n, KY, TL), BF),
            pltpu.VMEM((2, 2, 2, NZ, NY, KY, TL), BF),
            pltpu.VMEM((K, NB), BF),
            dma(()), dma((2,)), dma((2,)),
            dma((16,)),
            dma((2,)), dma((6,)),
            dma((2, 3, 2, 4)),
            dma((NZ + 2,)), dma((2, 2)), dma((2, 2, NZ)), dma((2, 2)),
            pltpu.SemaphoreType.REGULAR, pltpu.SemaphoreType.REGULAR((NY // 2, 2)),
        ],
        compiler_params=pltpu.CompilerParams(
            collective_id=0, has_side_effects=True, vmem_limit_bytes=60 * 1024 * 1024
        ),
        name="reflect",
    )(eigvecs, vt, factors)
    return out


def solution(mesh):
    in_specs = (P("rows", "vecs"), P(None, "rows", "vecs"), P())
    out_specs = P("rows", "vecs")
    return jax.shard_map(body, mesh=mesh, in_specs=in_specs, out_specs=out_specs, check_vma=False)
```

time: 695 us -> 89.9 us (0.13); the launches traced: 686 us -> 89.8 us
  blocking collectives: 575 us -> 0 us
  Pallas kernels: 0 us -> 89 us
  waiting for transfers between devices: 80.7 us -> 0 us
  between operations: 13.4 us -> 0.01 us
  matrix products: 12.5 us -> 0 us
    psum x2 -> x0, blocking collectives: 575 us -> none  [body(): coeff = lax.psum(partial_value, 'rows').astype(jnp.bfloat16)]
    pallas_call x0 -> x1, Pallas kernels: none -> 89 us  [body(): pl.pallas_call(kernel, out_shape=pltpu.VMEM((R, K), BF), in_specs=[hbm, h...]
    all_gather x2 -> x0, waiting for transfers between devices: 80 us -> none  [body(): panel = lax.all_gather(reflectors[which], 'vecs', axis=1, tiled=True)]
    dot_general x4 -> x0, matrix products: 12.5 us -> none  [the longest x2 7.43 us: body(): update = jnp.dot(panel, scaled, preferred_element_type=jnp.float32)]
  transfers between devices with their start and end apart: 2 -> 0, of which waited for: 1 -> 0; matrix products, arithmetic and copies ran while one was open for 1% -> 0% of each run, Pallas kernels for 0% -> 0%
where the time goes in v3:
time: 89.9 us; the launch traced here: 89.8 us
  Pallas kernels  89 us (99%)
    pallas_call x1, Pallas kernels, body(): pl.pallas_call(kernel, out_shape=pltpu.VMEM((R, K), BF), in_specs=[hbm, h...  89 us

profile of v3, /device:TPU:1, one launch (start us, length us, event | category | flops | bytes accessed | tf_op | source)
XLA Modules:
  0.0 89.8 jit_solution(12599746649424931407)
XLA Ops:
  0.0 89.0 %reflect.1 = bf16[1024,256]{1,0:T(8,128)(2,1)S(1)} custom-call(bf16[1024,256]{1,0:T(8,128)(2,1)} %e_ref.1, bf16[2,4,16,1024]{3,2,1,0:T(8,128)(2,1)} %bitcast.3, bf16[2,1024,1024]{2,1,0:T(8,128)(2,1)} %f_ref.1), custom_call_target="tpu_custom_call" | custom-call | tf_op jit(solution)/shard_map/reflect/pallas_call | solution.py:374
  89.0 0.8 copy.5

commit v4 on v3

--- a/solution.py
+++ b/solution.py
@@ -200,9 +200,8 @@
                 acc = t if acc is None else acc + t
             sc[:, i * T : (i + 1) * T] = acc.astype(BF)
 
-        @pl.loop(0, R // T)
-        def _(i):
-            lanes = pl.ds(pl.multiple_of(i * T, T), T)
+        for i in range(R // T):
+            lanes = slice(i * T, (i + 1) * T)
             v = vt[p, :, :, lanes].reshape(NB, T)
             upd = lax.dot_general(sc[...], v, NN, preferred_element_type=F32)
             new = (left[:, lanes].astype(F32) - upd).astype(BF)
@@ -229,8 +228,7 @@
             add1(n - 1)
 
     def partial0():
-        @pl.loop(0, NZ)
-        def _(i):
+        for i in range(NZ):
             partial(0, cur, i)
 
         for hf in (0, 1):
@@ -319,10 +317,9 @@
         forward(0, O, 2)
         forward(0, B, 3)
         forward(0, A, 3)
+        forward(0, O, 3)
     with scope("S19_spreadA"):
         spread(1, 0)
-    with scope("S20_v0"):
-        forward(0, O, 3)
     with scope("S21_spreadB"):
         spread(1, 1)
     with scope("S22_v0"):

time: 89.9 us -> 88.1 us (0.980)
  Pallas kernels: 89 us -> 87.2 us
    pallas_call x1, Pallas kernels: 89 us -> 87.2 us  [body(): pl.pallas_call(kernel, out_shape=pltpu.VMEM((R, K), BF), in_specs=[hbm, h...]
where the time goes in v4:
time: 88.1 us; the launch traced here: 88 us
  Pallas kernels  87.2 us (99%)
    pallas_call x1, Pallas kernels, body(): pl.pallas_call(kernel, out_shape=pltpu.VMEM((R, K), BF), in_specs=[hbm, h...  87.2 us

profile of v4, /device:TPU:1, one launch (start us, length us, event | category | flops | bytes accessed | tf_op | source)
XLA Modules:
  0.0 88.0 jit_solution(13311145370074385172)
XLA Ops:
  0.0 87.2 %reflect.1 = bf16[1024,256]{1,0:T(8,128)(2,1)S(1)} custom-call(bf16[1024,256]{1,0:T(8,128)(2,1)} %e_ref.1, bf16[2,4,16,1024]{3,2,1,0:T(8,128)(2,1)} %bitcast.3, bf16[2,1024,1024]{2,1,0:T(8,128)(2,1)} %f_ref.1), custom_call_target="tpu_custom_call" | custom-call | tf_op jit(solution)/shard_map/reflect/pallas_call | solution.py:371
  87.2 0.8 copy.5
